TPU v7x, 32 devices: a whole 2x2x4 slice. The times are simulated.
32 devices in a mesh: outer: 8 (over z, core), inner: 4 (over y, x).
Axes of the slice: x: 2, y: 2, z: 4, core: 2. Of those that a mesh axis runs over, the one named last changes fastest.
Arguments:
- queries: bfloat16 [2048, 4096], P(('outer', 'inner')), may hold values from -6 to 6
- keys: bfloat16 [2048, 4096], P(('outer', 'inner')), may hold values from -6 to 6
- values: bfloat16 [2048, 4096], P(('outer', 'inner')), may hold values from -6 to 6
- lengths: int32 [16], replicated, may hold values from 1 to 32, 128 in all
- norm_gain: float32 [4096], replicated, may hold values from 0.5 to 1.5
Outputs:
- attended: bfloat16 [2048, 4096], P(('outer', 'inner'))
Inputs may be any that keep to these rules, and one draw needn't show every extreme that they name: The lengths sum to 128; one document is exactly 32 units long.
All inputs are finite; a program needn't handle non-finite values.
Results may differ from a plain program's by a relative error of at most 0.0049.
Values sent between devices are 32-bit elements; how exact they have to be, the bound alone decides.
No kernel may reach another device: no remote copies, remote signals or barrier semaphores. Data moves between devices by JAX's collectives and lax.ppermute only.
A program may use at most 64 MiB of HBM per device.

v0:
```python
import jax
import jax.numpy as jnp
from jax import lax
from jax.sharding import PartitionSpec as P

HEAD_DIM = 128
BLOCK = 16
EPSILON = 1e-05


def carried_in(shard, axis, combine, identity):
    devices, index = (lax.axis_size(axis), lax.axis_index(axis))
    everything = jax.tree.map(lambda part: lax.all_gather(part, axis), shard)
    start = jax.tree.map(
        lambda part, zero: jnp.broadcast_to(jnp.asarray(zero, part.dtype), part.shape),
        shard,
        identity,
    )

    def lap(k, before):
        reached = k < index
        new = combine(before, jax.tree.map(lambda part: part[k], everything))
        return jax.tree.map(lambda a, b: jnp.where(reached, a, b), new, before)

    return lax.fori_loop(0, devices, lap, start)


def join_states(earlier, later):
    return (jnp.maximum(earlier[0], later[0]), later[1] + (1.0 - later[0]) * earlier[1])


def doc_ids(tok_rows, doc_starts):
    return jnp.sum((tok_rows[:, None] >= doc_starts[None, :]).astype(jnp.int32), axis=1) - 1


def body(queries, keys, values, lengths, norm_gain):
    tok_count = queries.shape[0]
    head_count = queries.shape[1] // HEAD_DIM
    state_rows = head_count * HEAD_DIM
    inner_count = lax.axis_size("inner")
    share_rows = state_rows // inner_count
    inner_place = lax.axis_index("inner")
    outer_place = lax.axis_index("outer")
    device_place = outer_place * inner_count + inner_place
    first_row = device_place * tok_count
    tok_rows = first_row + jnp.arange(tok_count, dtype=jnp.int32)
    doc_starts = BLOCK * (jnp.cumsum(lengths) - lengths)
    docs = doc_ids(tok_rows, doc_starts)
    first_doc = docs[0]
    final_doc = docs[-1]
    opens_block = jnp.any(doc_starts == first_row).astype(jnp.float32)
    group_places = outer_place * inner_count + jnp.arange(inner_count, dtype=jnp.int32)
    group_first = group_places * tok_count
    block_flags = jnp.any(
        (doc_starts[None, :] >= group_first[:, None])
        & (doc_starts[None, :] < group_first[:, None] + tok_count),
        axis=1,
    ).astype(jnp.float32)
    query_heads = queries.reshape(tok_count, head_count, HEAD_DIM)
    key_heads = keys.reshape(tok_count, head_count, HEAD_DIM)
    value_heads = values.reshape(tok_count, head_count, HEAD_DIM)
    final_keys = jnp.where((docs == final_doc)[:, None, None], key_heads, jnp.zeros_like(key_heads))
    local_state = jnp.einsum(
        "thd,the->hde", final_keys, value_heads, preferred_element_type=jnp.float32
    )
    shares = lax.all_to_all(
        local_state.reshape(1, state_rows, HEAD_DIM),
        "inner",
        split_axis=1,
        concat_axis=0,
        tiled=True,
    )
    scores = jnp.einsum("thd,shd->hts", query_heads, key_heads, preferred_element_type=jnp.float32)
    allowed = (tok_rows[:, None] >= tok_rows[None, :]) & (docs[:, None] == docs[None, :])
    weights = jnp.where(allowed[None], scores, 0.0).astype(jnp.bfloat16)
    intra = jnp.einsum("hts,she->the", weights, value_heads, preferred_element_type=jnp.float32)

    def walk(carried, item):
        return (join_states(carried, item), carried)

    share_zero = (jnp.float32(0.0), jnp.zeros((share_rows, HEAD_DIM), jnp.float32))
    group_total, earlier_in_group = lax.scan(walk, share_zero, (block_flags, shares))
    outer_prefix = carried_in(group_total, "outer", join_states, share_zero)
    combined = (
        earlier_in_group[1] + (1.0 - earlier_in_group[0])[:, None, None] * outer_prefix[1][None]
    )
    returned = lax.all_to_all(combined, "inner", split_axis=0, concat_axis=1, tiled=True)
    prefix_state = returned.reshape(head_count, HEAD_DIM, HEAD_DIM)
    carry_in = (1.0 - opens_block) * prefix_state
    held = carry_in.astype(jnp.bfloat16)
    inter = jnp.einsum("thd,hde->the", query_heads, held, preferred_element_type=jnp.float32)
    inter = jnp.where((docs == first_doc)[:, None, None], inter, 0.0)
    mixed = intra + inter
    scale = lax.rsqrt(jnp.mean(mixed * mixed, axis=-1, keepdims=True) + EPSILON)
    gain_heads = norm_gain.reshape(head_count, HEAD_DIM)
    attended = (mixed * scale * gain_heads[None]).astype(jnp.bfloat16)
    return attended.reshape(tok_count, head_count * HEAD_DIM)


def solution(mesh):
    placed = (
        P(("outer", "inner"), None),
        P(("outer", "inner"), None),
        P(("outer", "inner"), None),
        P(),
        P(),
    )
    return jax.shard_map(
        body, mesh=mesh, in_specs=placed, out_specs=P(("outer", "inner"), None), check_vma=False
    )
```

profile of v0, /device:TPU:0, one launch (start us, length us, event | category | flops | bytes accessed | tf_op | source)
XLA Modules:
  0.0 167.0 jit_solution(1256728201418256629)
XLA Ops:
  6.5 0.0 copy-start
  6.5 0.8 copy.26
  7.4 0.1 reduce
  7.5 1.4 compare_reduce_fusion
  8.9 0.1 convert_reduce_fusion
  9.0 0.6 fusion.27
  9.6 1.3 broadcast_compare_fusion.1
  10.9 0.0 copy-done
  10.9 2.9 %fusion.5 = f32[32,128,128]{2,1,0:T(8,128)} fusion(pred[64]{0:T(512)(128)(4,1)S(1)} %get-tuple-element.213, bf16[64,4096]{1,0:T(8,128)(2,1)S(1)} %copy-done, bf16[64,4096]{1,0:T(8,128)(2,1)} %param.10), kind=kOutput, calls=%fused_computation.16 | convolution fusion | flops 67371008 | bytes 3145792 | tf_op jit(solution)/shard_map/thd,the->hde/dot_general | solution.py:63
  13.8 5.2 %all-to-all-start = ((f32[1,4096,128]{2,0,1:T(1,128)}), f32[1,4096,128]{2,0,1:T(1,128)S(1)}, u32[]{:S(2)}, u32[]{:S(2)}) async-start(f32[1,4096,128]{2,0,1:T(1,128)} %bitcast.90), calls=%async_computation | async-start | bytes 4194304 | tf_op jit(solution)/shard_map/all_to_all | solution.py:66
  19.0 0.2 and_reduce_fusion
  19.2 24.6 %all-to-all-done = f32[1,4096,128]{2,0,1:T(1,128)S(1)} async-done(((f32[1,4096,128]{2,0,1:T(1,128)}), f32[1,4096,128]{2,0,1:T(1,128)S(1)}, u32[]{:S(2)}, u32[]{:S(2)}) %all-to-all-start) | async-done | bytes 2097184 | tf_op jit(solution)/shard_map/all_to_all | solution.py:66
  43.8 12.1 %while.31 = (s32[]{:T(128)}, f32[]{:T(128)}, f32[1024,128]{1,0:T(8,128)S(1)}, f32[4]{0:T(128)S(1)}, f32[4,1024,128]{2,1,0:T(8,128)}, /*index=5*/f32[4]{0:T(128)S...) while((s32[]{:T(128)}, f32[]{:T(128)}, f32[1024,128]{1,0:T(8,128)S(1)}, ...), condition=%wide.region_5.6_spmd.clone, body=%wide.region_4.5_spmd.clone.sunk | while | flops 524293 | bytes 2622128 | solution.py:82
  43.8 0.8 bitcast_dynamic-update-slice_fusion.2
  44.7 0.6 dynamic_slice.33
  46.0 0.1 bitcast_add_fusion.3
  46.7 0.1 dynamic_update_slice.14
  46.8 0.8 bitcast_dynamic-update-slice_fusion.2
  47.7 0.6 dynamic_slice.33
  49.0 0.1 bitcast_add_fusion.3
  49.8 0.1 dynamic_update_slice.14
  49.9 0.8 bitcast_dynamic-update-slice_fusion.2
  50.7 0.6 dynamic_slice.33
  52.0 0.1 bitcast_add_fusion.3
  52.8 0.1 dynamic_update_slice.14
  52.9 0.8 bitcast_dynamic-update-slice_fusion.2
  53.7 0.6 dynamic_slice.33
  55.0 0.1 bitcast_add_fusion.3
  55.8 0.1 dynamic_update_slice.14
  55.9 0.8 copy-done.1
  56.7 0.0 all-gather.3.cloned.1.call-update
  56.8 0.7 dynamic-slice
  57.4 0.8 dynamic-update-slice
  58.2 16.4 %all-reduce = f32[8]{0:T(128)S(1)} all-reduce(f32[8]{0:T(128)S(1)} %dynamic-update-slice), channel_id=1, replica_groups=mesh['outer'=8,'inner'=4] {'outer'}, use_global_device_ids=true, to_apply=%add | all-reduce | flops 8 | bytes 64
  74.6 29.9 %all-gather.3.cloned.1.call-done = f32[8192,128]{1,0:T(8,128)} async-done(((f32[1024,128]{1,0:T(8,128)}), f32[8192,128]{1,0:T(8,128)}) %all-gather.3.cloned.1.call-update) | async-done | bytes 4194320 | tf_op jit(solution)/shard_map/all_gather | solution.py:13
  104.5 21.9 %while.32 = (s32[]{:T(128)}, f32[1024,128]{1,0:T(8,128)S(1)}, s32[]{:T(128)}, f32[8,1024,128]{2,1,0:T(8,128)}, f32[8]{0:T(128)S(1)}, /*index=5*/s32[]{:T(128)}, f32[1]{0:T(128)}, s32[]{:T(128)}) while((s32[]{:T(128)}, f32[1024,128]{1,0:T(8,128)S(1)}, s32[]{:T(128)}, f32[8,1024,128]{2,1,0:T(8,128)}, f32[8]{0:T(128)S(1)}, ...), condition=%wide.region_7.8_spmd.clone, body=%wide.region_6.7_spmd.clone.sunk | while | flops 524293 | bytes 1573001 | solution.py:25
  104.5 0.6 dynamic_slice.35
  105.8 1.5 fusion.37
  107.3 0.6 dynamic_slice.35
  108.5 1.5 fusion.37
  110.0 0.6 dynamic_slice.35
  111.2 1.5 fusion.37
  112.7 0.6 dynamic_slice.35
  114.0 1.5 fusion.37
  115.5 0.6 dynamic_slice.35
  116.7 1.5 fusion.37
  118.2 0.6 dynamic_slice.35
  119.5 1.5 fusion.37
  120.9 0.6 dynamic_slice.35
  122.2 1.5 fusion.37
  123.7 0.6 dynamic_slice.35
  124.9 1.5 fusion.37
  126.4 0.0 copy-done.2
  126.4 1.6 multiply_add_fusion
  128.0 4.0 %all-to-all-start.1 = ((f32[4,1024,128]{2,1,0:T(8,128)}), f32[4,1024,128]{2,1,0:T(8,128)S(1)}, u32[]{:S(2)}, u32[]{:S(2)}) async-start(f32[4,1024,128]{2,1,0:T(8,128)} %multiply_add_fusion), calls=%async_computation.1 | async-start | bytes 4194304 | tf_op jit(solution)/shard_map/all_to_all | solution.py:87
  132.6 0.1 compare_and_fusion
  132.7 0.0 copy-done.4
  132.7 2.6 %convolution_bitcast_fusion = f32[64,32,128]{2,0,1:T(8,128)} fusion(pred[64,64]{1,0:T(8,128)(4,1)S(1)} %compare_and_fusion, bf16[64,4096]{1,0:T(8,128)(2,1)S(1)} %copy-done, bf16[64,4096]{1,0:T(8,128)(2,1)S(1)} %copy-done.4, bf16[64,4096]{1,0:T(8,128)(2,1)} %param.9), kind=kOutput, calls=%fused_computation.10 | convolution fusion | flops 67371008 | bytes 2625536 | tf_op jit(solution)/shard_map/hts,she->the/dot_general | solution.py:76
  135.3 22.0 %all-to-all-done.1 = f32[4,1024,128]{2,1,0:T(8,128)S(1)} async-done(((f32[4,1024,128]{2,1,0:T(8,128)}), f32[4,1024,128]{2,1,0:T(8,128)S(1)}, u32[]{:S(2)}, u32[]{:S(2)}) %all-to-all-start.1) | async-done | bytes 2097184 | tf_op jit(solution)/shard_map/all_to_all | solution.py:87
  157.3 0.2 multiply_convert_fusion
  157.4 0.0 copy-start.6
  157.5 1.0 copy-done.3
  158.5 0.5 multiply_reduce_fusion
  159.0 1.1 copy_bitcast_fusion
  (22 shorter events, 0.1 us)
Async XLA Ops:
  6.5 4.3 %copy-start = (bf16[64,4096]{1,0:T(8,128)(2,1)S(1)}, bf16[64,4096]{1,0:T(8,128)(2,1)}, u32[]{:S(2)}) copy-start(bf16[64,4096]{1,0:T(8,128)(2,1)} %param.11) | copy-start | bytes 1572868
  13.8 30.0 %all-to-all-start = ((f32[1,4096,128]{2,0,1:T(1,128)}), f32[1,4096,128]{2,0,1:T(1,128)S(1)}, u32[]{:S(2)}, u32[]{:S(2)}) async-start(f32[1,4096,128]{2,0,1:T(1,128)} %bitcast.90), calls=%async_computation | async-start | bytes 4194304 | tf_op jit(solution)/shard_map/all_to_all | solution.py:66
  19.0 85.6 %all-gather.3.cloned.1.call-start = ((), (), s32[]{:S(2)}) async-start(), calls=%async_computation.2 | async-start | bytes 4718592 | tf_op jit(solution)/shard_map/all_gather | solution.py:13
  43.8 12.9 %copy-start.7 = (u32[32]{0:T(128)S(1)}, u32[32]{0:T(128)}, u32[]{:S(2)}) copy-start(u32[32]{0:T(128)} %constant.84) | copy-start | bytes 388
  55.9 0.8 copy-start.1
  55.9 70.5 %copy-start.2 = (f32[4,1024,128]{2,1,0:T(8,128)S(1)}, f32[4,1024,128]{2,1,0:T(8,128)}, u32[]{:S(2)}) copy-start(f32[4,1024,128]{2,1,0:T(8,128)} %get-tuple-element.139) | copy-start | bytes 6291460
  128.0 4.7 %copy-start.4 = (bf16[64,4096]{1,0:T(8,128)(2,1)S(1)}, bf16[64,4096]{1,0:T(8,128)(2,1)}, u32[]{:S(2)}) copy-start(bf16[64,4096]{1,0:T(8,128)(2,1)} %param.10) | copy-start | bytes 1572868
  128.0 29.3 %all-to-all-start.1 = ((f32[4,1024,128]{2,1,0:T(8,128)}), f32[4,1024,128]{2,1,0:T(8,128)S(1)}, u32[]{:S(2)}, u32[]{:S(2)}) async-start(f32[4,1024,128]{2,1,0:T(8,128)} %multiply_add_fusion), calls=%async_computation.1 | async-start | bytes 4194304 | tf_op jit(solution)/shard_map/all_to_all | solution.py:87
  135.3 22.2 %copy-start.5 = (bf16[64,4096]{1,0:T(8,128)(2,1)S(1)}, bf16[64,4096]{1,0:T(8,128)(2,1)}, u32[]{:S(2)}) copy-start(bf16[64,4096]{1,0:T(8,128)(2,1)} %param.9) | copy-start | bytes 1572868
  157.3 1.2 copy-start.3
  157.4 1.6 copy-start.6
Sparse Core Ops, SparseCore 0:
  56.8 47.6 all-gather.2
where the time goes:
time: 168 us; the launch traced here: 167 us
  waiting for transfers between devices  76.5 us (46%)
  other arithmetic  21.8 us (13%)
  blocking collectives  16.4 us (10%)
  between operations  14.2 us (8%)
  local copies, waits for them, and re-layouts  12.4 us (7%)
  loops' own time  10.5 us (6%)
  starting transfers between devices  9.12 us (5%)
  matrix products  6.03 us (4%)
    all_gather x1, waiting for transfers between devices, carried_in(): everything = jax.tree.map(lambda part: lax.all_gather(part, axis), shard)  29.9 us
    all_to_all x1, waiting for transfers between devices, body(): lax.all_to_all(local_state.reshape(1, state_rows, HEAD_DIM), 'inner', spl...  24.6 us
    all_to_all x1, waiting for transfers between devices, body(): lax.all_to_all(combined, 'inner', split_axis=0, concat_axis=1, tiled=True)  22 us
    unnamed x1, blocking collectives  16.4 us
    select_n x8, other arithmetic, lap(): return jax.tree.map(lambda a, b: jnp.where(reached, a, b), new, before)  11.8 us
    another operation x1, loops' own time, carried_in(): return lax.fori_loop(0, devices, lap, start)  5.38 us
    all_to_all x1, starting transfers between devices, body(): lax.all_to_all(local_state.reshape(1, state_rows, HEAD_DIM), 'inner', spl...  5.17 us
    another operation x1, loops' own time, body(): lax.scan(walk, share_zero, (block_flags, shares))  5.11 us
  transfers between devices with their start and end apart: 3, of which 3 were waited for; matrix products, arithmetic and copies ran while one was open for 3% of the time, Pallas kernels for 0%

commit v1 on v0

--- a/solution.py
+++ b/solution.py
@@ -6,6 +6,18 @@
 HEAD_DIM = 128
 BLOCK = 16
 EPSILON = 1e-05
+
+
+def in_blocks(shard, dim, count):
+    dims = shard.shape
+    tiles = shard.reshape(*dims[:dim], count, dims[dim] // count, *dims[dim + 1 :])
+    return jnp.moveaxis(tiles, dim, 0)
+
+
+def laid_out(blocks, dim):
+    blocks = jnp.moveaxis(blocks, 0, dim)
+    shape = blocks.shape
+    return blocks.reshape(*shape[:dim], shape[dim] * shape[dim + 1], *shape[dim + 2 :])
 
 
 def carried_in(shard, axis, combine, identity):
@@ -84,7 +96,14 @@
     combined = (
         earlier_in_group[1] + (1.0 - earlier_in_group[0])[:, None, None] * outer_prefix[1][None]
     )
-    returned = lax.all_to_all(combined, "inner", split_axis=0, concat_axis=1, tiled=True)
+    size, mine = (lax.axis_size("inner"), lax.axis_index("inner"))
+    parts = in_blocks(combined, 0, size)
+    outs = [parts[mine]]
+    for step in range(1, size):
+        sent = parts[mine ^ step]
+        outs.append(lax.ppermute(sent, "inner", [(i, i ^ step) for i in range(size)]))
+    parts = jnp.stack(outs)[mine ^ jnp.arange(size)]
+    returned = laid_out(parts, 1)
     prefix_state = returned.reshape(head_count, HEAD_DIM, HEAD_DIM)
     carry_in = (1.0 - opens_block) * prefix_state
     held = carry_in.astype(jnp.bfloat16)

time: 168 us -> 168 us (level)
  other arithmetic: 21.8 us -> 23.7 us
  local copies, waits for them, and re-layouts: 12.4 us -> 14.1 us
    all_to_all x1 -> x0, waiting for transfers between devices: 22 us -> none  [body(): lax.all_to_all(combined, 'inner', split_axis=0, concat_axis=1, tiled=True)]
    ppermute x0 -> x3, waiting for transfers between devices: none -> 20.7 us  [body(): lax.ppermute(sent, 'inner', [(i, i ^ step) for i in range(size)])]
    all_to_all x1 -> x0, starting transfers between devices: 3.96 us -> none  [body(): lax.all_to_all(combined, 'inner', split_axis=0, concat_axis=1, tiled=True)]
    ppermute x0 -> x3, starting transfers between devices: none -> 3.49 us  [body(): lax.ppermute(sent, 'inner', [(i, i ^ step) for i in range(size)])]
    gather x0 -> x1, local copies, waits for them, and re-layouts: none -> 2.01 us  [body(): parts = jnp.stack(outs)[mine ^ jnp.arange(size)]]
    convert_element_type x1, other arithmetic: 0.17 us -> 1.87 us  [body(): held = carry_in.astype(jnp.bfloat16)]
  transfers between devices with their start and end apart: 3 -> 5, of which waited for: 3 -> 5; matrix products, arithmetic and copies ran while one was open for 3% -> 2% of each run, Pallas kernels for 0% -> 0%
where the time goes in v1:
time: 168 us; the launch traced here: 167 us
  waiting for transfers between devices  75.4 us (45%)
  other arithmetic  23.7 us (14%)
  blocking collectives  16.4 us (10%)
  between operations  14.3 us (9%)
  local copies, waits for them, and re-layouts  14.1 us (8%)
  loops' own time  9.91 us (6%)
  starting transfers between devices  8.66 us (5%)
  matrix products  4.97 us (3%)
    all_gather x1, waiting for transfers between devices, carried_in(): everything = jax.tree.map(lambda part: lax.all_gather(part, axis), shard)  30 us
    all_to_all x1, waiting for transfers between devices, body(): lax.all_to_all(local_state.reshape(1, state_rows, HEAD_DIM), 'inner', spl...  24.6 us
    ppermute x3, waiting for transfers between devices, body(): lax.ppermute(sent, 'inner', [(i, i ^ step) for i in range(size)])  20.7 us
    unnamed x1, blocking collectives  16.4 us
    select_n x8, other arithmetic, lap(): return jax.tree.map(lambda a, b: jnp.where(reached, a, b), new, before)  11.8 us
    another operation x1, loops' own time, carried_in(): return lax.fori_loop(0, devices, lap, start)  5.38 us
    all_to_all x1, starting transfers between devices, body(): lax.all_to_all(local_state.reshape(1, state_rows, HEAD_DIM), 'inner', spl...  5.17 us
    dynamic_slice x8, local copies, waits for them, and re-layouts, lap(): new = combine(before, jax.tree.map(lambda part: part[k], everything))  4.69 us
  transfers between devices with their start and end apart: 5, of which 5 were waited for; matrix products, arithmetic and copies ran while one was open for 2% of the time, Pallas kernels for 0%

profile of v1, /device:TPU:0, one launch (start us, length us, event | category | flops | bytes accessed | tf_op | source)
XLA Modules:
  0.0 167.4 jit_solution(3239970305296384705)
XLA Ops:
  6.5 0.8 copy.26
  7.4 0.1 reduce
  7.5 1.4 compare_reduce_fusion
  8.9 0.1 convert_reduce_fusion
  9.0 0.6 fusion.28
  9.6 1.3 broadcast_compare_fusion.1
  10.8 2.9 %fusion.5 = f32[32,128,128]{2,1,0:T(8,128)} fusion(pred[64]{0:T(512)(128)(4,1)S(1)} %get-tuple-element.217, bf16[64,4096]{1,0:T(8,128)(2,1)S(1)} %copy-done, bf16[64,4096]{1,0:T(8,128)(2,1)} %param.10), kind=kOutput, calls=%fused_computation.18 | convolution fusion | flops 67371008 | bytes 3145792 | tf_op jit(solution)/shard_map/thd,the->hde/dot_general | solution.py:75
  13.8 5.2 %all-to-all-start = ((f32[1,4096,128]{2,0,1:T(1,128)}), f32[1,4096,128]{2,0,1:T(1,128)S(1)}, u32[]{:S(2)}, u32[]{:S(2)}) async-start(f32[1,4096,128]{2,0,1:T(1,128)} %bitcast.99), calls=%async_computation | async-start | bytes 4194304 | tf_op jit(solution)/shard_map/all_to_all | solution.py:78
  19.0 0.2 and_reduce_fusion
  19.2 24.6 %all-to-all-done = f32[1,4096,128]{2,0,1:T(1,128)S(1)} async-done(((f32[1,4096,128]{2,0,1:T(1,128)}), f32[1,4096,128]{2,0,1:T(1,128)S(1)}, u32[]{:S(2)}, u32[]{:S(2)}) %all-to-all-start) | async-done | bytes 2097184 | tf_op jit(solution)/shard_map/all_to_all | solution.py:78
  43.8 11.2 %while.31 = (s32[]{:T(128)}, f32[]{:T(128)}, f32[1024,128]{1,0:T(8,128)S(1)}, f32[4]{0:T(128)S(1)}, f32[4,1024,128]{2,1,0:T(8,128)}, /*index=5*/f32[4]{0:T(128)S...) while((s32[]{:T(128)}, f32[]{:T(128)}, f32[1024,128]{1,0:T(8,128)S(1)}, ...), condition=%wide.region_5.6_spmd.clone, body=%wide.region_4.5_spmd.clone.sunk | while | flops 524293 | bytes 2622128 | solution.py:94
  43.8 0.9 bitcast_dynamic-update-slice_fusion.2
  44.7 0.6 dynamic_slice.40
  45.8 0.1 bitcast_add_fusion.3
  46.5 0.1 dynamic_update_slice.14
  46.6 0.8 bitcast_dynamic-update-slice_fusion.2
  47.5 0.6 dynamic_slice.40
  48.6 0.1 bitcast_add_fusion.3
  49.3 0.1 dynamic_update_slice.14
  49.4 0.8 bitcast_dynamic-update-slice_fusion.2
  50.3 0.6 dynamic_slice.40
  51.4 0.1 bitcast_add_fusion.3
  52.1 0.1 dynamic_update_slice.14
  52.2 0.8 bitcast_dynamic-update-slice_fusion.2
  53.1 0.6 dynamic_slice.40
  54.2 0.1 bitcast_add_fusion.3
  54.9 0.1 dynamic_update_slice.14
  55.0 0.8 copy-done.1
  55.9 0.6 dynamic-slice.7
  56.5 0.7 dynamic-update-slice
  57.2 16.4 %all-reduce = f32[8]{0:T(128)S(1)} all-reduce(f32[8]{0:T(128)S(1)} %dynamic-update-slice), channel_id=1, replica_groups=mesh['outer'=8,'inner'=4] {'outer'}, use_global_device_ids=true, to_apply=%add | all-reduce | flops 8 | bytes 64
  73.7 30.0 %all-gather.3.cloned.1.call-done = f32[8192,128]{1,0:T(8,128)} async-done(((f32[1024,128]{1,0:T(8,128)}), f32[8192,128]{1,0:T(8,128)}) %all-gather.3.cloned.1.call-update) | async-done | bytes 4194320 | tf_op jit(solution)/shard_map/all_gather | solution.py:25
  103.7 21.9 %while.32 = (s32[]{:T(128)}, f32[1024,128]{1,0:T(8,128)S(1)}, s32[]{:T(128)}, f32[8,1024,128]{2,1,0:T(8,128)}, f32[8]{0:T(128)S(1)}, /*index=5*/s32[]{:T(128)}, f32[1]{0:T(128)}, s32[]{:T(128)}) while((s32[]{:T(128)}, f32[1024,128]{1,0:T(8,128)S(1)}, s32[]{:T(128)}, f32[8,1024,128]{2,1,0:T(8,128)}, f32[8]{0:T(128)S(1)}, ...), condition=%wide.region_7.8_spmd.clone, body=%wide.region_6.7_spmd.clone.sunk | while | flops 524293 | bytes 1573001 | solution.py:37
  103.7 0.6 dynamic_slice.42
  104.9 1.5 fusion.38
  106.4 0.6 dynamic_slice.42
  107.6 1.5 fusion.38
  109.1 0.6 dynamic_slice.42
  110.4 1.5 fusion.38
  111.9 0.6 dynamic_slice.42
  113.1 1.5 fusion.38
  114.6 0.6 dynamic_slice.42
  115.8 1.5 fusion.38
  117.3 0.6 dynamic_slice.42
  118.6 1.5 fusion.38
  120.1 0.6 dynamic_slice.42
  121.3 1.5 fusion.38
  122.8 0.6 dynamic_slice.42
  124.0 1.5 fusion.38
  125.5 0.2 multiply_add_fusion
  125.8 0.9 dynamic-slice_bitcast_fusion
  126.8 1.4 collective-permute-start
  128.2 1.7 %collective-permute-start.1 = (f32[1,1024,128]{2,1,0:T(8,128)S(1)}, f32[1,1024,128]{2,1,0:T(8,128)}, u32[]{:S(2)}, u32[]{:S(2)}) collective-permute-start(f32[1,1024,128]{2,1,0:T(8,128)S(1)} %get-tuple-element.214), channel_id=1, source_target_pairs={{0,2},{1,3},{2,0},{3,1},{4,6},{5,7},{6,4},{7,5},{8,10},{9,11},{10,... | collective-permute-start | bytes 1572872 | tf_op jit(solution)/shard_map/ppermute | solution.py:104
  129.9 0.3 collective-permute-start.2
  131.1 1.6 convolution_bitcast_fusion
  132.6 9.2 %collective-permute-done = f32[1,1024,128]{2,1,0:T(8,128)} collective-permute-done((f32[1,1024,128]{2,1,0:T(8,128)}, f32[1,1024,128]{2,1,0:T(8,128)}, u32[]{:S(2)}, u32[]{:S(2)}) %collective-permute-start) | collective-permute-done | bytes 524320 | tf_op jit(solution)/shard_map/ppermute | solution.py:104
  141.8 10.6 %collective-permute-done.1 = f32[1,1024,128]{2,1,0:T(8,128)} collective-permute-done((f32[1,1024,128]{2,1,0:T(8,128)S(1)}, f32[1,1024,128]{2,1,0:T(8,128)}, u32[]{:S(2)}, u32[]{:S(2)}) %collective-permute-start.1) | collective-permute-done | bytes 524320 | tf_op jit(solution)/shard_map/ppermute | solution.py:104
  152.5 0.8 collective-permute-done.2
  153.3 1.5 maximum_bitcast_fusion
  154.8 2.0 %gather_fusion = f32[4,1024,128]{2,1,0:T(8,128)} fusion(f32[4,1024,128]{2,1,0:T(8,128)S(1)} %maximum_bitcast_fusion, s32[1024]{0:T(1024)S(1)} %pad_clamp_fusion), kind=kCustom, calls=%fused_computation | custom fusion | bytes 4194320 | tf_op jit(solution)/shard_map/gather | solution.py:105
  156.8 1.9 %multiply_convert_fusion = bf16[4,1024,128]{2,1,0:T(8,128)(2,1)S(1)} fusion(f32[4,1024,128]{2,1,0:T(8,128)} %gather_fusion, f32[]{:T(128)S(6)} %sub.28), kind=kLoop, calls=%fused_computation.6 | loop fusion | flops 1048576 | bytes 3145732 | tf_op jit(solution)/shard_map/convert_element_type | solution.py:109
  158.8 0.5 multiply_reduce_fusion
  159.3 0.1 copy-done.7
  159.4 1.1 copy_bitcast_fusion
  (33 shorter events, 0.3 us)
Async XLA Ops:
  6.5 4.3 %copy-start = (bf16[64,4096]{1,0:T(8,128)(2,1)S(1)}, bf16[64,4096]{1,0:T(8,128)(2,1)}, u32[]{:S(2)}) copy-start(bf16[64,4096]{1,0:T(8,128)(2,1)} %param.11) | copy-start | bytes 1572868
  13.8 30.0 %all-to-all-start = ((f32[1,4096,128]{2,0,1:T(1,128)}), f32[1,4096,128]{2,0,1:T(1,128)S(1)}, u32[]{:S(2)}, u32[]{:S(2)}) async-start(f32[1,4096,128]{2,0,1:T(1,128)} %bitcast.99), calls=%async_computation | async-start | bytes 4194304 | tf_op jit(solution)/shard_map/all_to_all | solution.py:78
  18.9 84.7 %all-gather.3.cloned.1.call-start = ((), (), s32[]{:S(2)}) async-start(), calls=%async_computation.1 | async-start | bytes 4718592 | tf_op jit(solution)/shard_map/all_gather | solution.py:25
  43.8 12.1 %copy-start.8 = (u32[32]{0:T(128)S(1)}, u32[32]{0:T(128)}, u32[]{:S(2)}) copy-start(u32[32]{0:T(128)} %constant.92) | copy-start | bytes 388
  55.0 0.8 copy-start.1
  55.0 70.5 %copy-start.2 = (f32[4,1024,128]{2,1,0:T(8,128)S(1)}, f32[4,1024,128]{2,1,0:T(8,128)}, u32[]{:S(2)}) copy-start(f32[4,1024,128]{2,1,0:T(8,128)} %get-tuple-element.139) | copy-start | bytes 6291460
  125.8 5.3 %copy-start.4 = (bf16[64,4096]{1,0:T(8,128)(2,1)S(1)}, bf16[64,4096]{1,0:T(8,128)(2,1)}, u32[]{:S(2)}) copy-start(bf16[64,4096]{1,0:T(8,128)(2,1)} %param.10) | copy-start | bytes 1572868
  125.8 5.2 %copy-start.5 = (bf16[64,4096]{1,0:T(8,128)(2,1)S(1)}, bf16[64,4096]{1,0:T(8,128)(2,1)}, u32[]{:S(2)}) copy-start(bf16[64,4096]{1,0:T(8,128)(2,1)} %param.9) | copy-start | bytes 1572868
  126.8 15.1 %collective-permute-start = (f32[1,1024,128]{2,1,0:T(8,128)}, f32[1,1024,128]{2,1,0:T(8,128)}, u32[]{:S(2)}, u32[]{:S(2)}) collective-permute-start(f32[1,1024,128]{2,1,0:T(8,128)} %get-tuple-element.215), channel_id=1, source_target_pairs={{0,1},{1,0},{2,3},{3,2},{4,5},{5,4},{6,7},{7,6},{8,9},{9,8},{10,11... | collective-permute-start | bytes 1572872 | tf_op jit(solution)/shard_map/ppermute | solution.py:104
  128.2 24.3 %collective-permute-start.1 = (f32[1,1024,128]{2,1,0:T(8,128)S(1)}, f32[1,1024,128]{2,1,0:T(8,128)}, u32[]{:S(2)}, u32[]{:S(2)}) collective-permute-start(f32[1,1024,128]{2,1,0:T(8,128)S(1)} %get-tuple-element.214), channel_id=1, source_target_pairs={{0,2},{1,3},{2,0},{3,1},{4,6},{5,7},{6,4},{7,5},{8,10},{9,11},{10,... | collective-permute-start | bytes 1572872 | tf_op jit(solution)/shard_map/ppermute | solution.py:104
  129.9 23.4 %collective-permute-start.2 = (f32[1,1024,128]{2,1,0:T(8,128)S(1)}, f32[1,1024,128]{2,1,0:T(8,128)}, u32[]{:S(2)}, u32[]{:S(2)}) collective-permute-start(f32[1,1024,128]{2,1,0:T(8,128)S(1)} %get-tuple-element.213), channel_id=1, source_target_pairs={{0,3},{1,2},{2,1},{3,0},{4,7},{5,6},{6,5},{7,4},{8,11},{9,10},{10,... | collective-permute-start | bytes 1572872 | tf_op jit(solution)/shard_map/ppermute | solution.py:104
  156.8 1.9 %copy-start.3 = (f32[64,32,128]{2,0,1:T(8,128)S(1)}, f32[64,32,128]{2,0,1:T(8,128)}, u32[]{:S(2)}) copy-start(f32[64,32,128]{2,0,1:T(8,128)} %convolution_bitcast_fusion) | copy-start | bytes 3145732
  156.8 2.0 %copy-start.6 = (bf16[64,4096]{1,0:T(8,128)(2,1)S(1)}, bf16[64,4096]{1,0:T(8,128)(2,1)}, u32[]{:S(2)}) copy-start(bf16[64,4096]{1,0:T(8,128)(2,1)} %param.9) | copy-start | bytes 1572868
  158.7 0.7 copy-start.7
Sparse Core Ops, SparseCore 0:
  56.0 47.6 all-gather.2
